TPU v7x, 256 devices: a whole 4x4x8 slice. The times are simulated.
256 devices in a mesh: slab: 32 (over x, z_hi, y), head: 8 (over z_lo, core).
Axes of the slice: x: 4, y: 4, z: 8 (z_hi: 2, z_lo: 4; z = z_hi * 4 + z_lo), core: 2. Of those that a mesh axis runs over, the one named last changes fastest.
Arguments:
- inputs: bfloat16 [32768, 1024], P('slab'), may hold values from -6 to 6
- norm_gain: float32 [1024], replicated, may hold values from 0.1 to 1.9
- query_weight: bfloat16 [1024, 1024], P('slab', 'head'), may hold values from -0.1875 to 0.1875
- key_weight: bfloat16 [1024, 1024], P('slab', 'head'), may hold values from -0.1875 to 0.1875
- value_weight: bfloat16 [1024, 1024], P('slab', 'head'), may hold values from -0.1875 to 0.1875
- out_weight: bfloat16 [1024, 1024], P('head', 'slab'), may hold values from -0.1875 to 0.1875
- logit_scale: float32 [16], P('head'), may hold values from 0.5 to 4, as said below
- grad_output: bfloat16 [32768, 1024], P('slab'), may hold values from -6 to 6
Outputs:
- grad_inputs: bfloat16 [32768, 1024], P('slab', 'head')
- grad_gain: float32 [1024], P('head')
- grad_query_weight: float32 [1024, 1024], P('slab', 'head')
- grad_key_weight: float32 [1024, 1024], P('slab', 'head')
- grad_value_weight: float32 [1024, 1024], P('slab', 'head')
- grad_out_weight: float32 [1024, 1024], P('head', 'slab')
Inputs may be any that keep to these rules, and one draw needn't show every extreme that they name: `logit_scale`: positive multipliers of each head's attention logits.
All inputs are finite; a program needn't handle non-finite values.
Results may differ from a plain program's by a relative error of at most 0.015.
The roundings to bfloat16 on the way count: a program that leaves them out, or rounds other values in their place, can miss the bound.
Values may be sent and summed in bfloat16 or wider, within the bound.
No kernel may reach another device: no remote copies, remote signals or barrier semaphores. Data moves between devices by JAX's collectives and lax.ppermute only.
A program may use at most 128 MiB of HBM per device.

v0:
```python
import math
import jax
import jax.numpy as jnp
from jax import lax
from jax.sharding import PartitionSpec as P

NX = 32
NY = 32


def rows_first(arrays, axis, dims):
    turned = [jnp.moveaxis(a, dim, 0) for a, dim in zip(arrays, dims)]
    widths = [t[0].size for t in turned]
    both = jnp.concatenate([t.reshape(-1, w) for t, w in zip(turned, widths)], axis=1)
    whole = lax.all_gather(both, axis, axis=0, tiled=True)
    pieces = jnp.split(whole, [sum(widths[:k]) for k in range(1, len(widths))], axis=1)
    return tuple(
        (
            jnp.moveaxis(b.reshape(-1, *t.shape[1:]), 0, dim)
            for b, t, dim in zip(pieces, turned, dims)
        )
    )


def sent_together(arrays, axis, split_dim, concat_dim, along):
    both = jnp.concatenate(arrays, axis=along)
    whole, at, done = (
        lax.all_to_all(both, axis, split_axis=split_dim, concat_axis=concat_dim, tiled=True),
        0,
        [],
    )
    for a in arrays:
        done.append(lax.slice_in_dim(whole, at, at + a.shape[along], axis=along))
        at += a.shape[along]
    return tuple(done)


def shortened(x):

    def short(part):
        return part.astype(jnp.bfloat16) if part.dtype == jnp.float32 else part

    return jax.tree.map(short, x)


def split_up(x, dim, size):
    lengths = x.shape
    pieces = x.reshape(*lengths[:dim], size, lengths[dim] // size, *lengths[dim + 1 :])
    return jnp.moveaxis(pieces, dim, 0)


def summed_on_arrival(x, axis, dim):
    size = lax.axis_size(axis)
    pieces = lax.all_to_all(split_up(x, dim, size), axis, 0, 0, tiled=True)
    return jnp.sum(pieces.astype(jnp.float32), axis=0)


def sent_to_all(x, axis):
    size = lax.axis_size(axis)
    return lax.all_to_all(jnp.broadcast_to(x[None], (size, *x.shape)), axis, 0, 0, tiled=True)


def over_copies(x, axis):
    everything = sent_to_all(x, axis)
    return jnp.sum(everything, axis=0)


def summed_on_arrival_2(x, axis, dim):
    size = lax.axis_size(axis)
    pieces = lax.all_to_all(split_up(x, dim, size), axis, 0, 0, tiled=True)
    return jnp.sum(pieces, axis=0)


def line_attention(queries, key_rows, values, grad_attn, scale_factor):
    line_count, length, head_count, head_dim = queries.shape
    bundle = math.gcd(line_count, max(1, 128 // length))
    block_width = length * bundle
    blocks = line_count // bundle
    query_blocks, key_blocks, value_blocks, grad_blocks = tuple(
        (
            tensor.reshape(blocks, block_width, head_count, head_dim)
            for tensor in (queries, key_rows, values, grad_attn)
        )
    )
    position = jnp.arange(block_width) // length
    same_line = position[:, None] == position[None, :]
    factor = scale_factor[None, :, None, None]
    score_matrix = (
        jnp.einsum("bqhd,bkhd->bhqk", query_blocks, key_blocks, preferred_element_type=jnp.float32)
        * factor
    )
    score_matrix = jnp.where(same_line, score_matrix, -jnp.inf)
    highest = jnp.max(score_matrix, axis=-1, keepdims=True)
    exponent = jnp.exp(score_matrix - highest)
    softmax_p = exponent / jnp.sum(exponent, axis=-1, keepdims=True)
    rounded_probability = softmax_p.astype(jnp.bfloat16)
    output_rows = jnp.einsum(
        "bhqk,bkhd->bqhd", rounded_probability, value_blocks, preferred_element_type=jnp.float32
    )
    probability_gradient = jnp.einsum(
        "bqhd,bkhd->bhqk", grad_blocks, value_blocks, preferred_element_type=jnp.float32
    )
    row_delta = jnp.einsum("bqhd,bqhd->bhq", grad_blocks.astype(jnp.float32), output_rows)
    score_gradient = (softmax_p * (probability_gradient - row_delta[..., None]) * factor).astype(
        jnp.bfloat16
    )
    query_gradient = jnp.einsum(
        "bhqk,bkhd->bqhd", score_gradient, key_blocks, preferred_element_type=jnp.float32
    )
    key_gradient = jnp.einsum(
        "bhqk,bqhd->bkhd", score_gradient, query_blocks, preferred_element_type=jnp.float32
    )
    value_gradient = jnp.einsum(
        "bhqk,bqhd->bkhd", rounded_probability, grad_blocks, preferred_element_type=jnp.float32
    )
    return tuple(
        (
            result.reshape(line_count, length, head_count, head_dim)
            for result in (output_rows, query_gradient, key_gradient, value_gradient)
        )
    )


def local_axes(grids, scale_factor, head_dim):
    planes, rows_y, rows_x, head_width = grids[0].shape
    head_count = head_width // head_dim
    along_x = line_attention(
        *[grid.reshape(planes * rows_y, rows_x, head_count, head_dim) for grid in grids],
        scale_factor
    )
    along_x = [result.reshape(planes, rows_y, rows_x, head_width) for result in along_x]
    along_y = line_attention(
        *[
            jnp.transpose(grid, (0, 2, 1, 3)).reshape(planes * rows_x, rows_y, head_count, head_dim)
            for grid in grids
        ],
        scale_factor
    )
    along_y = [
        jnp.transpose(result.reshape(planes, rows_x, rows_y, head_width), (0, 2, 1, 3))
        for result in along_y
    ]
    return tuple((along_x[index] + along_y[index] for index in range(4)))


def z_lines(grids, scale_factor, head_dim):
    depth, rows_y, rows_x, head_width = grids[0].shape
    head_count = head_width // head_dim
    results = line_attention(
        *[
            jnp.transpose(grid, (1, 2, 0, 3)).reshape(rows_y * rows_x, depth, head_count, head_dim)
            for grid in grids
        ],
        scale_factor
    )
    return tuple(
        (
            jnp.transpose(result.reshape(rows_y, rows_x, depth, head_width), (2, 0, 1, 3)).astype(
                jnp.bfloat16
            )
            for result in results
        )
    )


def body(
    inputs, norm_gain, query_weight, key_weight, value_weight, out_weight, logit_scale, grad_output
):
    rows, width = inputs.shape
    head_width = query_weight.shape[1]
    head_dim = head_width // logit_scale.shape[0]
    slab_count = lax.axis_size("slab")
    share = width // lax.axis_size("head")
    loss_scale = 1.0 / math.sqrt(rows * slab_count)
    planes = rows // (NY * NX)
    features = inputs.astype(jnp.float32)
    inv_rms = lax.rsqrt(jnp.mean(features * features, axis=1) + 1e-06)
    normed = (features * inv_rms[:, None] * norm_gain[None, :]).astype(jnp.bfloat16)
    full_query, full_key, full_value, full_out = rows_first(
        (query_weight, key_weight, value_weight, out_weight), "slab", (0, 0, 0, 1)
    )
    queries = jnp.dot(normed, full_query, preferred_element_type=jnp.float32).astype(jnp.bfloat16)
    key_rows = jnp.dot(normed, full_key, preferred_element_type=jnp.float32).astype(jnp.bfloat16)
    values = jnp.dot(normed, full_value, preferred_element_type=jnp.float32).astype(jnp.bfloat16)
    grad_attn = lax.dot_general(
        grad_output, full_out, (((1,), (1,)), ((), ())), preferred_element_type=jnp.float32
    ).astype(jnp.bfloat16)
    scale_factor = logit_scale / math.sqrt(head_dim)
    grids = tuple(
        (
            array.reshape(planes, NY, NX, head_width)
            for array in (queries, key_rows, values, grad_attn)
        )
    )
    moved = sent_together((grids[0], grids[1], grids[2]), "slab", 1, 0, 2)
    moved_grad = lax.all_to_all(grids[3], "slab", split_axis=1, concat_axis=0, tiled=True)
    z_terms = z_lines((moved[0], moved[1], moved[2], moved_grad), scale_factor, head_dim)
    z_back = jax.tree.map(
        lambda part, own: part.astype(own.dtype),
        lax.all_to_all(shortened(z_terms), "slab", split_axis=0, concat_axis=1, tiled=True),
        z_terms,
    )
    local_terms = local_axes(grids, scale_factor, head_dim)
    combined = tuple(
        (
            (local_terms[index] + z_back[index].astype(jnp.float32))
            .astype(jnp.bfloat16)
            .reshape(rows, head_width)
            for index in range(4)
        )
    )
    attn, query_gradient, key_gradient, value_gradient = combined
    contract = (((1,), (1,)), ((), ()))
    partial_sum = lax.dot_general(
        query_gradient, full_query, contract, preferred_element_type=jnp.float32
    )
    partial_sum = partial_sum + lax.dot_general(
        key_gradient, full_key, contract, preferred_element_type=jnp.float32
    )
    partial_sum = partial_sum + lax.dot_general(
        value_gradient, full_value, contract, preferred_element_type=jnp.float32
    )
    partial_sum = partial_sum.astype(jnp.bfloat16)
    first_col = lax.axis_index("head") * share
    feature_share = lax.dynamic_slice_in_dim(features, first_col, share, 1)
    gain_share = lax.dynamic_slice_in_dim(norm_gain, first_col, share, 0)
    grad_normed = summed_on_arrival(partial_sum, "head", 1)
    row_dot = over_copies(
        jnp.sum(grad_normed * feature_share * gain_share[None, :], axis=1), "head"
    )
    grad_inputs = (
        inv_rms[:, None] * gain_share[None, :] * grad_normed
        - feature_share * (inv_rms**3)[:, None] * row_dot[:, None] / width
    ).astype(jnp.bfloat16)
    grad_gain = (
        over_copies(jnp.sum(grad_normed * feature_share * inv_rms[:, None], axis=0), "slab")
        * loss_scale
    )
    grads_stack = jnp.concatenate([query_gradient, key_gradient, value_gradient], axis=1)
    tokens_contract = (((0,), (0,)), ((), ()))
    inner = lax.dot_general(
        normed, grads_stack, tokens_contract, preferred_element_type=jnp.float32
    )
    outer = lax.dot_general(grad_output, attn, tokens_contract, preferred_element_type=jnp.float32)
    reduced = summed_on_arrival_2(jnp.concatenate([inner, outer], axis=1), "slab", 0) * loss_scale
    grad_query_weight = reduced[:, :head_width]
    grad_key_weight = reduced[:, head_width : 2 * head_width]
    grad_value_weight = reduced[:, 2 * head_width : 3 * head_width]
    grad_out_weight = reduced[:, 3 * head_width :].T
    return (
        grad_inputs,
        grad_gain,
        grad_query_weight,
        grad_key_weight,
        grad_value_weight,
        grad_out_weight,
    )


def solution(mesh):
    in_specs = (
        P("slab", None),
        P(),
        P("slab", "head"),
        P("slab", "head"),
        P("slab", "head"),
        P("head", "slab"),
        P("head"),
        P("slab", None),
    )
    out_specs = (
        P("slab", "head"),
        P("head"),
        P("slab", "head"),
        P("slab", "head"),
        P("slab", "head"),
        P("head", "slab"),
    )
    return jax.shard_map(body, mesh=mesh, in_specs=in_specs, out_specs=out_specs, check_vma=False)
```

profile of v0, /device:TPU:72, one launch (start us, length us, event | category | flops | bytes accessed | tf_op | source)
XLA Modules:
  0.0 466.1 jit_solution(10997156738980183589)
XLA Ops:
  8.8 4.0 copy.273
  12.8 2.2 multiply_reduce_fusion
  15.1 1.9 multiply_convert_fusion
  17.0 75.5 %all-gather.2.cloned.1.call-done = bf16[1024,512]{1,0:T(8,128)(2,1)} async-done(((bf16[32,512]{1,0:T(8,128)(2,1)}), bf16[1024,512]{1,0:T(8,128)(2,1)}) %all-gather.2.cloned.1.call-update) | async-done | bytes 1048592 | tf_op jit(solution)/shard_map/all_gather | solution.py:15
  92.5 1.8 convolution_convert_fusion.4
  98.8 2.4 convolution_convert_fusion.5
  103.6 2.4 convolution_convert_fusion.6
  108.3 3.0 convolution_convert_fusion.3
  111.3 2.1 reshape.205
  115.2 2.0 reshape_reshape.56
  117.2 1.9 copy.295
  120.3 2.7 fusion.65
  122.9 2.4 fusion.35
  125.4 1.8 fusion.19
  129.5 7.8 %all-to-all-start.1 = ((bf16[1,32,32,128]{3,2,0,1:T(8,128)(2,1)}), bf16[1,32,32,128]{3,2,0,1:T(8,128)(2,1)}, u32[]{:S(2)}, u32[]{:S(2)}) async-start(bf16[1,32,32,128]{3,2,0,1:T(8,128)(2,1)} %bitcast.29), calls=%async_computation.1 | async-start | bytes 524288 | tf_op jit(solution)/shard_map/all_to_all | solution.py:196
  138.6 2.0 copy.284
  141.3 1.9 copy.280
  144.2 2.7 convolution_bitcast_fusion.1
  148.4 2.6 all-to-all-done.1
  151.1 9.7 %all-to-all-start = ((bf16[1,32,96,128]{3,2,0,1:T(8,128)(2,1)}), bf16[1,32,96,128]{3,2,0,1:T(8,128)(2,1)S(1)}, u32[]{:S(2)}, u32[]{:S(2)}) async-start(bf16[1,32,96,128]{3,2,0,1:T(8,128)(2,1)} %pad_maximum_fusion.1), calls=%async_computation | async-start | bytes 1572864 | tf_op jit(solution)/shard_map/all_to_all | solution.py:28
  160.8 1.8 bitcast_convert_fusion.3
  162.6 2.6 fusion.36
  165.2 1.8 fusion.20
  174.7 2.1 copy.382
  176.8 7.7 %all-to-all-done = bf16[1,32,96,128]{3,2,0,1:T(8,128)(2,1)S(1)} async-done(((bf16[1,32,96,128]{3,2,0,1:T(8,128)(2,1)}), bf16[1,32,96,128]{3,2,0,1:T(8,128)(2,1)S(1)}, u32[]{:S(2)}, u32[]{:S(2)}) %all-to-all-start) | async-done | bytes 786464 | tf_op jit(solution)/shard_map/all_to_all | solution.py:28
  188.8 2.5 fusion.66
  192.8 1.9 fusion.34
  199.3 1.8 copy.333
  201.1 5.3 %all-to-all-start.3 = ((bf16[32,1,32,128]{3,2,1,0:T(8,128)(2,1)}), bf16[32,1,32,128]{3,2,1,0:T(8,128)(2,1)}, u32[]{:S(2)}, u32[]{:S(2)}) async-start(bf16[32,1,32,128]{3,2,1,0:T(8,128)(2,1)} %copy.333), calls=%async_computation.3 | async-start | bytes 524288 | tf_op jit(solution)/shard_map/all_to_all | solution.py:200
  206.4 2.6 convolution_bitcast_fusion.2
  210.4 1.8 reshape_reshape.65
  212.2 2.2 copy.337
  214.4 2.6 reshape_reshape.64
  217.0 2.2 copy.328
  219.2 2.6 reshape_reshape.63
  221.8 2.2 copy.325
  224.0 2.6 reshape_reshape.62
  226.7 2.2 copy.301
  228.8 2.7 reshape_reshape.57
  231.5 2.2 copy.286
  233.7 2.6 reshape_reshape.52
  244.6 2.0 copy.352
  248.7 12.3 %all-to-all-start.2 = ((bf16[32,1,32,128]{3,2,1,0:T(8,128)(2,1)}), bf16[32,1,32,128]{3,2,1,0:T(8,128)(2,1)}, u32[]{:S(2)}, u32[]{:S(2)}) async-start(bf16[32,1,32,128]{3,2,1,0:T(8,128)(2,1)} %copy.321), calls=%async_computation.2 | async-start | bytes 524288 | tf_op jit(solution)/shard_map/all_to_all | solution.py:200
  262.4 3.7 fusion.46
  266.1 8.1 %all-to-all-done.2 = bf16[32,1,32,128]{3,2,1,0:T(8,128)(2,1)} async-done(((bf16[32,1,32,128]{3,2,1,0:T(8,128)(2,1)}), bf16[32,1,32,128]{3,2,1,0:T(8,128)(2,1)}, u32[]{:S(2)}, u32[]{:S(2)}) %all-to-all-start.2) | async-done | bytes 262176 | tf_op jit(solution)/shard_map/all_to_all | solution.py:200
  274.2 5.3 %all-to-all-start.4 = ((bf16[32,1,32,128]{3,2,1,0:T(8,128)(2,1)}), bf16[32,1,32,128]{3,2,1,0:T(8,128)(2,1)}, u32[]{:S(2)}, u32[]{:S(2)}) async-start(bf16[32,1,32,128]{3,2,1,0:T(8,128)(2,1)} %copy.345), calls=%async_computation.4 | async-start | bytes 524288 | tf_op jit(solution)/shard_map/all_to_all | solution.py:200
  281.6 3.7 fusion.43
  285.3 6.5 %all-to-all-done.4 = bf16[32,1,32,128]{3,2,1,0:T(8,128)(2,1)} async-done(((bf16[32,1,32,128]{3,2,1,0:T(8,128)(2,1)}), bf16[32,1,32,128]{3,2,1,0:T(8,128)(2,1)}, u32[]{:S(2)}, u32[]{:S(2)}) %all-to-all-start.4) | async-done | bytes 262176 | tf_op jit(solution)/shard_map/all_to_all | solution.py:200
  291.9 5.9 %all-to-all-start.8 = ((bf16[32,1,32,128]{3,2,1,0:T(8,128)(2,1)}), bf16[32,1,32,128]{3,2,1,0:T(8,128)(2,1)}, u32[]{:S(2)}, u32[]{:S(2)}) async-start(bf16[32,1,32,128]{3,2,1,0:T(8,128)(2,1)} %copy.353), calls=%async_computation.8 | async-start | bytes 524288 | tf_op jit(solution)/shard_map/all_to_all | solution.py:200
  299.7 5.6 %add_convert_fusion = bf16[1024,1024]{0,1:T(8,128)(2,1)} fusion(f32[1024,1024]{0,1:T(8,128)} %fusion.43, f32[1024,1024]{0,1:T(8,128)} %fusion.46, bf16[1024,128]{1,0:T(8,128)(2,1)S(1)} %bitcast.227, bf16[1024,512]{1,0:T(8,128)(2,1)} %all-gather.2.cloned.1.call-done), kind=kOutput, calls=%fused_computation.4 | convolution fusion | flops 271581184 | bytes 11010048 | tf_op jit(solution)/shard_map/dot_general | solution.py:220
  305.3 4.7 %all-to-all-done.8 = bf16[32,1,32,128]{3,2,1,0:T(8,128)(2,1)} async-done(((bf16[32,1,32,128]{3,2,1,0:T(8,128)(2,1)}), bf16[32,1,32,128]{3,2,1,0:T(8,128)(2,1)}, u32[]{:S(2)}, u32[]{:S(2)}) %all-to-all-start.8) | async-done | bytes 262176 | tf_op jit(solution)/shard_map/all_to_all | solution.py:200
  310.0 4.5 all-to-all-start.5
  314.5 4.0 convert_element_type.164
  324.4 2.3 fusion.30
  326.7 3.9 fusion.24
  330.6 29.4 %all-to-all-done.5 = bf16[8,1024,128]{1,2,0:T(8,128)(2,1)} async-done(((bf16[8,1024,128]{1,2,0:T(8,128)(2,1)}), bf16[8,1024,128]{1,2,0:T(8,128)(2,1)}, u32[]{:S(2)}, u32[]{:S(2)}) %all-to-all-start.5) | async-done | bytes 2097184 | tf_op jit(solution)/shard_map/all_to_all | solution.py:54
  359.9 2.0 convert_reduce_fusion
  363.8 7.5 %all-to-all-start.7 = ((f32[32,1,128]{2,1,0:T(1,128)}), f32[32,1,128]{2,1,0:T(1,128)S(1)}, u32[]{:S(2)}, u32[]{:S(2)}) async-start(f32[32,1,128]{2,1,0:T(1,128)} %broadcast_in_dim.23), calls=%async_computation.7 | async-start | bytes 32768 | tf_op jit(solution)/shard_map/all_to_all | solution.py:60
  371.8 10.5 %all-to-all-done.7 = f32[32,1,128]{2,1,0:T(1,128)S(1)} async-done(((f32[32,1,128]{2,1,0:T(1,128)}), f32[32,1,128]{2,1,0:T(1,128)S(1)}, u32[]{:S(2)}, u32[]{:S(2)}) %all-to-all-start.7) | async-done | bytes 16416 | tf_op jit(solution)/shard_map/all_to_all | solution.py:60
  382.9 6.6 %all-to-all-start.6 = ((f32[8,1,1024]{2,1,0:T(1,128)}), f32[8,1,1024]{2,1,0:T(1,128)S(1)}, u32[]{:S(2)}, u32[]{:S(2)}) async-start(f32[8,1,1024]{2,1,0:T(1,128)} %broadcast_in_dim.22), calls=%async_computation.6 | async-start | bytes 65536 | tf_op jit(solution)/shard_map/all_to_all | solution.py:60
  389.5 3.0 pad_maximum_fusion
  392.5 2.9 copy.355
  395.4 5.8 %all-to-all-start.9 = ((f32[32,32,512]{2,1,0:T(8,128)}), f32[32,32,512]{2,1,0:T(8,128)}, u32[]{:S(2)}, u32[]{:S(2)}) async-start(f32[32,32,512]{2,1,0:T(8,128)} %bitcast.201), calls=%async_computation.9 | async-start | bytes 4194304 | tf_op jit(solution)/shard_map/all_to_all | solution.py:70
  403.8 53.1 %all-to-all-done.9 = f32[32,32,512]{2,1,0:T(8,128)} async-done(((f32[32,32,512]{2,1,0:T(8,128)}), f32[32,32,512]{2,1,0:T(8,128)}, u32[]{:S(2)}, u32[]{:S(2)}) %all-to-all-start.9) | async-done | bytes 2097184 | tf_op jit(solution)/shard_map/all_to_all | solution.py:70
  (152 shorter events, 69.6 us)
Async XLA Ops:
  7.2 85.3 %copy-start = (bf16[1024,1024]{1,0:T(8,128)(2,1)S(1)}, bf16[1024,1024]{1,0:T(8,128)(2,1)}, u32[]{:S(2)}) copy-start(bf16[1024,1024]{1,0:T(8,128)(2,1)} %param.15) | copy-start | bytes 6291460
  7.2 85.3 %all-gather.2.cloned.1.call-start = ((), (), s32[]{:S(2)}) async-start(), calls=%async_computation.10 | async-start | bytes 1081344 | tf_op jit(solution)/shard_map/all_gather | solution.py:15
  8.8 4.0 copy-start.34
  12.7 2.4 copy-start.1
  12.7 2.4 copy-start.33
  101.2 4.8 %copy-start.3 = (bf16[1024,128]{1,0:T(8,128)(2,1)}, bf16[1024,128]{1,0:T(8,128)(2,1)S(1)}, u32[]{:S(2)}) copy-start(bf16[1024,128]{1,0:T(8,128)(2,1)S(1)} %convolution_convert_fusion.5) | copy-start | bytes 786436
  105.9 2.4 copy-start.5
  111.3 7.7 %copy-start.2 = (f32[8,2,128,64]{3,1,2,0:T(2,128)S(1)}, f32[8,2,128,64]{3,1,2,0:T(2,128)}, u32[]{:S(2)}) copy-start(f32[8,2,128,64]{3,1,2,0:T(2,128)} %bitcast_convert_fusion.2) | copy-start | bytes 1572868
  120.2 2.7 copy-start.17
  120.2 2.7 copy-start.19
  120.3 2.7 copy-start.32
  128.4 14.8 %copy-start.4 = (bf16[1024,128]{1,0:T(8,128)(2,1)S(1)}, bf16[1024,128]{1,0:T(8,128)(2,1)}, u32[]{:S(2)}) copy-start(bf16[1024,128]{1,0:T(8,128)(2,1)} %copy-done.3) | copy-start | bytes 786436
  128.4 14.8 %copy-start.6 = (bf16[1024,128]{1,0:T(8,128)(2,1)S(1)}, bf16[1024,128]{1,0:T(8,128)(2,1)}, u32[]{:S(2)}) copy-start(bf16[1024,128]{1,0:T(8,128)(2,1)} %copy-done.5) | copy-start | bytes 786436
  128.4 14.8 %copy-start.7 = (bf16[1024,128]{1,0:T(8,128)(2,1)S(1)}, bf16[1024,128]{1,0:T(8,128)(2,1)}, u32[]{:S(2)}) copy-start(bf16[1024,128]{1,0:T(8,128)(2,1)} %convolution_convert_fusion.3) | copy-start | bytes 786436
  129.5 21.6 %all-to-all-start.1 = ((bf16[1,32,32,128]{3,2,0,1:T(8,128)(2,1)}), bf16[1,32,32,128]{3,2,0,1:T(8,128)(2,1)}, u32[]{:S(2)}, u32[]{:S(2)}) async-start(bf16[1,32,32,128]{3,2,0,1:T(8,128)(2,1)} %bitcast.29), calls=%async_computation.1 | async-start | bytes 524288 | tf_op jit(solution)/shard_map/all_to_all | solution.py:196
  138.6 8.3 %copy-start.13 = (bf16[8,128,2,64]{1,3,2,0:T(8,128)(2,1)}, bf16[8,128,2,64]{1,3,2,0:T(8,128)(2,1)S(1)}, u32[]{:S(2)}) copy-start(bf16[8,128,2,64]{1,3,2,0:T(8,128)(2,1)S(1)} %copy.276) | copy-start | bytes 786436
  141.3 2.9 copy-start.18
  144.2 2.7 copy-start.16
  148.4 14.2 %copy-start.14 = (bf16[8,128,2,64]{1,3,2,0:T(8,128)(2,1)S(1)}, bf16[8,128,2,64]{1,3,2,0:T(8,128)(2,1)}, u32[]{:S(2)}) copy-start(bf16[8,128,2,64]{1,3,2,0:T(8,128)(2,1)} %copy-done.13) | copy-start | bytes 786436
  151.1 33.4 %all-to-all-start = ((bf16[1,32,96,128]{3,2,0,1:T(8,128)(2,1)}), bf16[1,32,96,128]{3,2,0,1:T(8,128)(2,1)S(1)}, u32[]{:S(2)}, u32[]{:S(2)}) async-start(bf16[1,32,96,128]{3,2,0,1:T(8,128)(2,1)} %pad_maximum_fusion.1), calls=%async_computation | async-start | bytes 1572864 | tf_op jit(solution)/shard_map/all_to_all | solution.py:28
  185.3 1.3 copy-start.29
  185.3 2.1 copy-start.28
  187.4 3.9 copy-start.23
  187.8 5.0 %copy-start.11 = (f32[8,2,128,64]{2,3,1,0:T(8,128)S(1)}, f32[8,2,128,64]{2,3,1,0:T(8,128)}, u32[]{:S(2)}) copy-start(f32[8,2,128,64]{2,3,1,0:T(8,128)} %copy.382) | copy-start | bytes 1572868
  191.3 3.4 copy-start.20
  191.3 3.4 copy-start.21
  191.3 3.4 copy-start.27
  194.7 1.2 copy-start.26
  195.1 0.8 copy-start.12
  195.9 10.5 %copy-start.15 = (bf16[8,128,2,64]{1,3,2,0:T(8,128)(2,1)S(1)}, bf16[8,128,2,64]{1,3,2,0:T(8,128)(2,1)}, u32[]{:S(2)}) copy-start(bf16[8,128,2,64]{1,3,2,0:T(8,128)(2,1)} %copy-done.13) | copy-start | bytes 786436
  201.1 47.6 %all-to-all-start.3 = ((bf16[32,1,32,128]{3,2,1,0:T(8,128)(2,1)}), bf16[32,1,32,128]{3,2,1,0:T(8,128)(2,1)}, u32[]{:S(2)}, u32[]{:S(2)}) async-start(bf16[32,1,32,128]{3,2,1,0:T(8,128)(2,1)} %copy.333), calls=%async_computation.3 | async-start | bytes 524288 | tf_op jit(solution)/shard_map/all_to_all | solution.py:200
  206.4 2.7 copy-start.31
  228.8 7.5 %copy-start.22 = (bf16[8,128,2,64]{1,3,2,0:T(8,128)(2,1)S(1)}, bf16[8,128,2,64]{1,3,2,0:T(8,128)(2,1)}, u32[]{:S(2)}) copy-start(bf16[8,128,2,64]{1,3,2,0:T(8,128)(2,1)} %copy.313) | copy-start | bytes 786436
  242.4 18.6 %copy-start.10 = (f32[1,32,32,128]{3,2,1,0:T(8,128)S(1)}, f32[1,32,32,128]{3,2,1,0:T(8,128)}, u32[]{:S(2)}) copy-start(f32[1,32,32,128]{3,2,1,0:T(8,128)} %reshape_reshape.63) | copy-start | bytes 1572868
  248.7 25.5 %all-to-all-start.2 = ((bf16[32,1,32,128]{3,2,1,0:T(8,128)(2,1)}), bf16[32,1,32,128]{3,2,1,0:T(8,128)(2,1)}, u32[]{:S(2)}, u32[]{:S(2)}) async-start(bf16[32,1,32,128]{3,2,1,0:T(8,128)(2,1)} %copy.321), calls=%async_computation.2 | async-start | bytes 524288 | tf_op jit(solution)/shard_map/all_to_all | solution.py:200
  262.4 17.1 %copy-start.9 = (f32[1,32,32,128]{3,2,1,0:T(8,128)S(1)}, f32[1,32,32,128]{3,2,1,0:T(8,128)}, u32[]{:S(2)}) copy-start(f32[1,32,32,128]{3,2,1,0:T(8,128)} %reshape_reshape.57) | copy-start | bytes 1572868
  274.2 17.7 %all-to-all-start.4 = ((bf16[32,1,32,128]{3,2,1,0:T(8,128)(2,1)}), bf16[32,1,32,128]{3,2,1,0:T(8,128)(2,1)}, u32[]{:S(2)}, u32[]{:S(2)}) async-start(bf16[32,1,32,128]{3,2,1,0:T(8,128)(2,1)} %copy.345), calls=%async_computation.4 | async-start | bytes 524288 | tf_op jit(solution)/shard_map/all_to_all | solution.py:200
  280.9 0.7 copy-start.24
  281.6 16.1 %copy-start.8 = (f32[1,32,32,128]{3,2,1,0:T(8,128)S(1)}, f32[1,32,32,128]{3,2,1,0:T(8,128)}, u32[]{:S(2)}) copy-start(f32[1,32,32,128]{3,2,1,0:T(8,128)} %reshape_reshape.64) | copy-start | bytes 1572868
  291.9 18.1 %all-to-all-start.8 = ((bf16[32,1,32,128]{3,2,1,0:T(8,128)(2,1)}), bf16[32,1,32,128]{3,2,1,0:T(8,128)(2,1)}, u32[]{:S(2)}, u32[]{:S(2)}) async-start(bf16[32,1,32,128]{3,2,1,0:T(8,128)(2,1)} %copy.353), calls=%async_computation.8 | async-start | bytes 524288 | tf_op jit(solution)/shard_map/all_to_all | solution.py:200
  299.0 0.7 copy-start.25
  310.0 50.0 %all-to-all-start.5 = ((bf16[8,1024,128]{1,2,0:T(8,128)(2,1)}), bf16[8,1024,128]{1,2,0:T(8,128)(2,1)}, u32[]{:S(2)}, u32[]{:S(2)}) async-start(bf16[8,1024,128]{1,2,0:T(8,128)(2,1)} %bitcast.202), calls=%async_computation.5 | async-start | bytes 4194304 | tf_op jit(solution)/shard_map/all_to_all | solution.py:54
  330.6 40.7 %copy-start.30 = (bf16[1,32,32,128]{3,2,1,0:T(8,128)(2,1)S(1)}, bf16[1,32,32,128]{3,2,1,0:T(8,128)(2,1)}, u32[]{:S(2)}) copy-start(bf16[1,32,32,128]{3,2,1,0:T(8,128)(2,1)} %fusion.30) | copy-start | bytes 786436
  363.8 18.5 %all-to-all-start.7 = ((f32[32,1,128]{2,1,0:T(1,128)}), f32[32,1,128]{2,1,0:T(1,128)S(1)}, u32[]{:S(2)}, u32[]{:S(2)}) async-start(f32[32,1,128]{2,1,0:T(1,128)} %broadcast_in_dim.23), calls=%async_computation.7 | async-start | bytes 32768 | tf_op jit(solution)/shard_map/all_to_all | solution.py:60
  382.9 12.5 %all-to-all-start.6 = ((f32[8,1,1024]{2,1,0:T(1,128)}), f32[8,1,1024]{2,1,0:T(1,128)S(1)}, u32[]{:S(2)}, u32[]{:S(2)}) async-start(f32[8,1,1024]{2,1,0:T(1,128)} %broadcast_in_dim.22), calls=%async_computation.6 | async-start | bytes 65536 | tf_op jit(solution)/shard_map/all_to_all | solution.py:60
  395.4 61.5 %all-to-all-start.9 = ((f32[32,32,512]{2,1,0:T(8,128)}), f32[32,32,512]{2,1,0:T(8,128)}, u32[]{:S(2)}, u32[]{:S(2)}) async-start(f32[32,32,512]{2,1,0:T(8,128)} %bitcast.201), calls=%async_computation.9 | async-start | bytes 4194304 | tf_op jit(solution)/shard_map/all_to_all | solution.py:70
Sparse Core Ops, SparseCore 0:
  12.0 80.4 all-gather.1
where the time goes:
time: 469 us; the launch traced here: 466 us
  waiting for transfers between devices  198 us (42%)
  local copies, waits for them, and re-layouts  91.6 us (20%)
  starting transfers between devices  70.8 us (15%)
  matrix products  58.1 us (12%)
  other arithmetic  32.8 us (7%)
  between operations  14.7 us (3%)
    all_gather x1, waiting for transfers between devices, rows_first(): whole = lax.all_gather(both, axis, axis=0, tiled=True)  75.5 us
    all_to_all x1, waiting for transfers between devices, summed_on_arrival_2(): pieces = lax.all_to_all(split_up(x, dim, size), axis, 0, 0, tiled=True)  53.1 us
    all_to_all x1, waiting for transfers between devices, summed_on_arrival(): pieces = lax.all_to_all(split_up(x, dim, size), axis, 0, 0, tiled=True)  29.4 us
    all_to_all x4, starting transfers between devices, body(): lax.all_to_all(shortened(z_terms), 'slab', split_axis=0, concat_axis=1, t...  28.7 us
    another operation x22, local copies, waits for them, and re-layouts, line_attention(): tensor.reshape(blocks, block_width, head_count, head_dim)  22.1 us
    all_to_all x4, waiting for transfers between devices, body(): lax.all_to_all(shortened(z_terms), 'slab', split_axis=0, concat_axis=1, t...  19.3 us
    all_to_all x2, starting transfers between devices, sent_to_all(): lax.all_to_all(jnp.broadcast_to(x[None], (size, *x.shape)), axis, 0, 0, t...  14.2 us
    convert_element_type x12, local copies, waits for them, and re-layouts, z_lines(): jnp.transpose(result.reshape(rows_y, rows_x, depth, head_width), (2, 0, 1...  13.7 us
  transfers between devices with their start and end apart: 11, of which 9 were waited for; matrix products, arithmetic and copies ran while one was open for 26% of the time, Pallas kernels for 0%

commit v1 on v0

--- a/solution.py
+++ b/solution.py
@@ -12,7 +12,9 @@
     turned = [jnp.moveaxis(a, dim, 0) for a, dim in zip(arrays, dims)]
     widths = [t[0].size for t in turned]
     both = jnp.concatenate([t.reshape(-1, w) for t, w in zip(turned, widths)], axis=1)
-    whole = lax.all_gather(both, axis, axis=0, tiled=True)
+    whole = jnp.concatenate(
+        lax.all_to_all(jnp.stack([both] * lax.axis_size(axis)), axis, 0, 0), axis=0
+    )
     pieces = jnp.split(whole, [sum(widths[:k]) for k in range(1, len(widths))], axis=1)
     return tuple(
         (

time: 469 us -> 411 us (0.88)
  waiting for transfers between devices: 198 us -> 141 us
  starting transfers between devices: 70.8 us -> 84.7 us
  between operations: 14.7 us -> 1.2 us
    all_gather x1 -> x0, waiting for transfers between devices: 75.5 us -> none  [rows_first(): whole = lax.all_gather(both, axis, axis=0, tiled=True)]
    all_to_all x0 -> x1, waiting for transfers between devices: none -> 23 us  [rows_first(): lax.all_to_all(jnp.stack([both] * lax.axis_size(axis)), axis, 0, 0)]
    all_to_all x0 -> x1, starting transfers between devices: none -> 12.4 us  [rows_first(): lax.all_to_all(jnp.stack([both] * lax.axis_size(axis)), axis, 0, 0)]
    unnamed x75 -> x83, local copies, waits for them, and re-layouts: 11.1 us -> 11.2 us
  transfers between devices with their start and end apart: 11 -> 11, of which waited for: 9 -> 9; matrix products, arithmetic and copies ran while one was open for 26% -> 28% of each run, Pallas kernels for 0% -> 0%
where the time goes in v1:
time: 411 us; the launch traced here: 409 us
  waiting for transfers between devices  141 us (34%)
  local copies, waits for them, and re-layouts  95 us (23%)
  starting transfers between devices  84.7 us (21%)
  matrix products  54.3 us (13%)
  other arithmetic  32.8 us (8%)
    all_to_all x1, waiting for transfers between devices, summed_on_arrival_2(): pieces = lax.all_to_all(split_up(x, dim, size), axis, 0, 0, tiled=True)  53.1 us
    all_to_all x4, starting transfers between devices, body(): lax.all_to_all(shortened(z_terms), 'slab', split_axis=0, concat_axis=1, t...  31.2 us
    all_to_all x1, waiting for transfers between devices, summed_on_arrival(): pieces = lax.all_to_all(split_up(x, dim, size), axis, 0, 0, tiled=True)  29.4 us
    another operation x22, local copies, waits for them, and re-layouts, line_attention(): tensor.reshape(blocks, block_width, head_count, head_dim)  25.7 us
    all_to_all x1, waiting for transfers between devices, rows_first(): lax.all_to_all(jnp.stack([both] * lax.axis_size(axis)), axis, 0, 0)  23 us
    all_to_all x4, waiting for transfers between devices, body(): lax.all_to_all(shortened(z_terms), 'slab', split_axis=0, concat_axis=1, t...  19.9 us
    all_to_all x2, starting transfers between devices, sent_to_all(): lax.all_to_all(jnp.broadcast_to(x[None], (size, *x.shape)), axis, 0, 0, t...  14.5 us
    all_to_all x1, starting transfers between devices, rows_first(): lax.all_to_all(jnp.stack([both] * lax.axis_size(axis)), axis, 0, 0)  12.4 us
  transfers between devices with their start and end apart: 11, of which 9 were waited for; matrix products, arithmetic and copies ran while one was open for 28% of the time, Pallas kernels for 0%

profile of v1, /device:TPU:72, one launch (start us, length us, event | category | flops | bytes accessed | tf_op | source)
XLA Modules:
  0.0 408.8 jit_solution(6394064291323753247)
XLA Ops:
  2.6 12.4 %all-to-all-start = ((bf16[32,32,512]{2,1,0:T(8,128)(2,1)}), bf16[32,32,512]{2,1,0:T(8,128)(2,1)S(1)}, u32[]{:S(2)}, u32[]{:S(2)}) async-start(bf16[32,32,512]{2,1,0:T(8,128)(2,1)} %stack.2), calls=%async_computation | async-start | bytes 2097152 | tf_op jit(solution)/shard_map/all_to_all | solution.py:16
  15.0 4.0 copy.273
  19.0 2.2 multiply_reduce_fusion
  21.3 1.9 multiply_convert_fusion
  23.2 23.0 %all-to-all-done = bf16[32,32,512]{2,1,0:T(8,128)(2,1)S(1)} async-done(((bf16[32,32,512]{2,1,0:T(8,128)(2,1)}), bf16[32,32,512]{2,1,0:T(8,128)(2,1)S(1)}, u32[]{:S(2)}, u32[]{:S(2)}) %all-to-all-start) | async-done | bytes 1048608 | tf_op jit(solution)/shard_map/all_to_all | solution.py:16
  46.2 3.5 convolution_convert_fusion.5
  63.9 2.1 reshape_reshape.53
  66.1 1.9 copy.299
  67.9 2.0 reshape.211
  69.9 1.8 copy.410
  71.7 2.0 reshape_reshape.56
  73.7 1.9 copy.295
  76.7 2.6 fusion.65
  79.4 2.4 fusion.35
  81.8 1.8 fusion.19
  86.0 5.2 %all-to-all-start.2 = ((bf16[1,32,32,128]{3,2,0,1:T(8,128)(2,1)}), bf16[1,32,32,128]{3,2,0,1:T(8,128)(2,1)}, u32[]{:S(2)}, u32[]{:S(2)}) async-start(bf16[1,32,32,128]{3,2,0,1:T(8,128)(2,1)} %bitcast.30), calls=%async_computation.2 | async-start | bytes 524288 | tf_op jit(solution)/shard_map/all_to_all | solution.py:198
  92.5 2.0 copy.284
  95.2 1.9 copy.280
  98.1 2.6 convolution_bitcast_fusion.1
  103.5 11.1 %all-to-all-start.1 = ((bf16[1,32,96,128]{3,2,0,1:T(8,128)(2,1)}), bf16[1,32,96,128]{3,2,0,1:T(8,128)(2,1)S(1)}, u32[]{:S(2)}, u32[]{:S(2)}) async-start(bf16[1,32,96,128]{3,2,0,1:T(8,128)(2,1)} %pad_maximum_fusion.1), calls=%async_computation.1 | async-start | bytes 1572864 | tf_op jit(solution)/shard_map/all_to_all | solution.py:30
  114.6 1.8 bitcast_convert_fusion.3
  116.4 2.6 fusion.36
  119.0 1.8 fusion.20
  123.1 1.8 copy.311
  128.4 2.1 copy.382
  130.6 3.9 all-to-all-done.1
  138.8 2.5 fusion.66
  142.7 1.9 fusion.34
  149.3 1.8 copy.333
  151.1 8.3 %all-to-all-start.4 = ((bf16[32,1,32,128]{3,2,1,0:T(8,128)(2,1)}), bf16[32,1,32,128]{3,2,1,0:T(8,128)(2,1)}, u32[]{:S(2)}, u32[]{:S(2)}) async-start(bf16[32,1,32,128]{3,2,1,0:T(8,128)(2,1)} %copy.333), calls=%async_computation.4 | async-start | bytes 524288 | tf_op jit(solution)/shard_map/all_to_all | solution.py:202
  159.4 2.6 convolution_bitcast_fusion.2
  163.3 2.7 reshape_reshape.65
  166.0 2.2 copy.337
  168.2 2.7 reshape_reshape.64
  172.1 2.7 reshape_reshape.63
  174.8 2.2 copy.325
  177.0 2.6 reshape_reshape.62
  180.9 2.7 reshape_reshape.57
  183.6 2.2 copy.286
  185.8 2.7 reshape_reshape.52
  192.0 2.0 fusion.21
  199.5 12.3 %all-to-all-start.3 = ((bf16[32,1,32,128]{3,2,1,0:T(8,128)(2,1)}), bf16[32,1,32,128]{3,2,1,0:T(8,128)(2,1)}, u32[]{:S(2)}, u32[]{:S(2)}) async-start(bf16[32,1,32,128]{3,2,1,0:T(8,128)(2,1)} %copy.321), calls=%async_computation.3 | async-start | bytes 524288 | tf_op jit(solution)/shard_map/all_to_all | solution.py:202
  213.4 2.7 fusion.46
  216.0 8.0 %all-to-all-done.3 = bf16[32,1,32,128]{3,2,1,0:T(8,128)(2,1)} async-done(((bf16[32,1,32,128]{3,2,1,0:T(8,128)(2,1)}), bf16[32,1,32,128]{3,2,1,0:T(8,128)(2,1)}, u32[]{:S(2)}, u32[]{:S(2)}) %all-to-all-start.3) | async-done | bytes 262176 | tf_op jit(solution)/shard_map/all_to_all | solution.py:202
  224.0 5.3 %all-to-all-start.5 = ((bf16[32,1,32,128]{3,2,1,0:T(8,128)(2,1)}), bf16[32,1,32,128]{3,2,1,0:T(8,128)(2,1)}, u32[]{:S(2)}, u32[]{:S(2)}) async-start(bf16[32,1,32,128]{3,2,1,0:T(8,128)(2,1)} %copy.345), calls=%async_computation.5 | async-start | bytes 524288 | tf_op jit(solution)/shard_map/all_to_all | solution.py:202
  231.6 2.7 fusion.43
  234.3 7.3 %all-to-all-done.5 = bf16[32,1,32,128]{3,2,1,0:T(8,128)(2,1)} async-done(((bf16[32,1,32,128]{3,2,1,0:T(8,128)(2,1)}), bf16[32,1,32,128]{3,2,1,0:T(8,128)(2,1)}, u32[]{:S(2)}, u32[]{:S(2)}) %all-to-all-start.5) | async-done | bytes 262176 | tf_op jit(solution)/shard_map/all_to_all | solution.py:202
  241.7 5.3 %all-to-all-start.9 = ((bf16[32,1,32,128]{3,2,1,0:T(8,128)(2,1)}), bf16[32,1,32,128]{3,2,1,0:T(8,128)(2,1)}, u32[]{:S(2)}, u32[]{:S(2)}) async-start(bf16[32,1,32,128]{3,2,1,0:T(8,128)(2,1)} %copy.353), calls=%async_computation.9 | async-start | bytes 524288 | tf_op jit(solution)/shard_map/all_to_all | solution.py:202
  249.3 5.5 %add_convert_fusion = bf16[1024,1024]{0,1:T(8,128)(2,1)} fusion(f32[1024,1024]{0,1:T(8,128)} %fusion.43, f32[1024,1024]{0,1:T(8,128)} %fusion.46, bf16[1024,128]{1,0:T(8,128)(2,1)S(1)} %bitcast.235, bf16[1024,512]{1,0:T(8,128)(2,1)S(1)} %bitcast.210), kind=kOutput, calls=%fused_computation.4 | convolution fusion | flops 271581184 | bytes 11010048 | tf_op jit(solution)/shard_map/dot_general | solution.py:222
  254.8 4.5 %all-to-all-done.9 = bf16[32,1,32,128]{3,2,1,0:T(8,128)(2,1)} async-done(((bf16[32,1,32,128]{3,2,1,0:T(8,128)(2,1)}), bf16[32,1,32,128]{3,2,1,0:T(8,128)(2,1)}, u32[]{:S(2)}, u32[]{:S(2)}) %all-to-all-start.9) | async-done | bytes 262176 | tf_op jit(solution)/shard_map/all_to_all | solution.py:202
  259.3 4.5 %all-to-all-start.6 = ((bf16[8,1024,128]{1,2,0:T(8,128)(2,1)}), bf16[8,1024,128]{1,2,0:T(8,128)(2,1)}, u32[]{:S(2)}, u32[]{:S(2)}) async-start(bf16[8,1024,128]{1,2,0:T(8,128)(2,1)} %bitcast.203), calls=%async_computation.6 | async-start | bytes 4194304 | tf_op jit(solution)/shard_map/all_to_all | solution.py:56
  263.8 4.0 convert_element_type.164
  273.7 2.3 fusion.30
  276.0 3.9 fusion.24
  279.9 29.4 %all-to-all-done.6 = bf16[8,1024,128]{1,2,0:T(8,128)(2,1)} async-done(((bf16[8,1024,128]{1,2,0:T(8,128)(2,1)}), bf16[8,1024,128]{1,2,0:T(8,128)(2,1)}, u32[]{:S(2)}, u32[]{:S(2)}) %all-to-all-start.6) | async-done | bytes 2097184 | tf_op jit(solution)/shard_map/all_to_all | solution.py:56
  309.2 2.0 convert_reduce_fusion
  313.1 7.8 %all-to-all-start.8 = ((f32[32,1,128]{2,1,0:T(1,128)}), f32[32,1,128]{2,1,0:T(1,128)S(1)}, u32[]{:S(2)}, u32[]{:S(2)}) async-start(f32[32,1,128]{2,1,0:T(1,128)} %broadcast_in_dim.23), calls=%async_computation.8 | async-start | bytes 32768 | tf_op jit(solution)/shard_map/all_to_all | solution.py:62
  321.4 10.5 %all-to-all-done.8 = f32[32,1,128]{2,1,0:T(1,128)S(1)} async-done(((f32[32,1,128]{2,1,0:T(1,128)}), f32[32,1,128]{2,1,0:T(1,128)S(1)}, u32[]{:S(2)}, u32[]{:S(2)}) %all-to-all-start.8) | async-done | bytes 16416 | tf_op jit(solution)/shard_map/all_to_all | solution.py:62
  332.5 6.6 %all-to-all-start.7 = ((f32[8,1,1024]{2,1,0:T(1,128)}), f32[8,1,1024]{2,1,0:T(1,128)S(1)}, u32[]{:S(2)}, u32[]{:S(2)}) async-start(f32[8,1,1024]{2,1,0:T(1,128)} %broadcast_in_dim.22), calls=%async_computation.7 | async-start | bytes 65536 | tf_op jit(solution)/shard_map/all_to_all | solution.py:62
  339.1 3.0 pad_maximum_fusion
  342.1 2.9 copy.355
  345.0 5.8 %all-to-all-start.10 = ((f32[32,32,512]{2,1,0:T(8,128)}), f32[32,32,512]{2,1,0:T(8,128)}, u32[]{:S(2)}, u32[]{:S(2)}) async-start(f32[32,32,512]{2,1,0:T(8,128)} %bitcast.202), calls=%async_computation.10 | async-start | bytes 4194304 | tf_op jit(solution)/shard_map/all_to_all | solution.py:72
  353.4 53.1 %all-to-all-done.10 = f32[32,32,512]{2,1,0:T(8,128)} async-done(((f32[32,32,512]{2,1,0:T(8,128)}), f32[32,32,512]{2,1,0:T(8,128)}, u32[]{:S(2)}, u32[]{:S(2)}) %all-to-all-start.10) | async-done | bytes 2097184 | tf_op jit(solution)/shard_map/all_to_all | solution.py:72
  406.5 1.7 reduce_sum.99
  (160 shorter events, 72.7 us)
Async XLA Ops:
  0.6 52.1 %copy-start = (bf16[1024,1024]{1,0:T(8,128)(2,1)S(1)}, bf16[1024,1024]{1,0:T(8,128)(2,1)}, u32[]{:S(2)}) copy-start(bf16[1024,1024]{1,0:T(8,128)(2,1)} %param.15) | copy-start | bytes 6291460
  2.6 43.6 %all-to-all-start = ((bf16[32,32,512]{2,1,0:T(8,128)(2,1)}), bf16[32,32,512]{2,1,0:T(8,128)(2,1)S(1)}, u32[]{:S(2)}, u32[]{:S(2)}) async-start(bf16[32,32,512]{2,1,0:T(8,128)(2,1)} %stack.2), calls=%async_computation | async-start | bytes 2097152 | tf_op jit(solution)/shard_map/all_to_all | solution.py:16
  15.0 4.0 copy-start.38
  19.0 2.3 copy-start.1
  19.0 2.4 copy-start.37
  46.2 6.5 %copy-start.2 = (bf16[32,32,512]{2,1,0:T(8,128)(2,1)}, bf16[32,32,512]{2,1,0:T(8,128)(2,1)S(1)}, u32[]{:S(2)}) copy-start(bf16[32,32,512]{2,1,0:T(8,128)(2,1)S(1)} %all-to-all-done) | copy-start | bytes 3145732
  46.2 3.5 copy-start.13
  53.5 4.5 %copy-start.5 = (bf16[1024,128]{1,0:T(8,128)(2,1)S(1)}, bf16[1024,128]{1,0:T(8,128)(2,1)}, u32[]{:S(2)}) copy-start(bf16[1024,128]{1,0:T(8,128)(2,1)} %convolution_convert_fusion.5) | copy-start | bytes 786436
  56.7 5.4 %copy-start.7 = (bf16[1024,128]{1,0:T(8,128)(2,1)S(1)}, bf16[1024,128]{1,0:T(8,128)(2,1)}, u32[]{:S(2)}) copy-start(bf16[1024,128]{1,0:T(8,128)(2,1)} %convolution_convert_fusion.6) | copy-start | bytes 786436
  63.9 11.6 %copy-start.4 = (f32[8,2,128,64]{3,1,2,0:T(2,128)S(1)}, f32[8,2,128,64]{3,1,2,0:T(2,128)}, u32[]{:S(2)}) copy-start(f32[8,2,128,64]{3,1,2,0:T(2,128)} %bitcast_convert_fusion.2) | copy-start | bytes 1572868
  76.7 2.6 copy-start.20
  76.7 2.6 copy-start.22
  76.7 2.6 copy-start.36
  84.9 12.2 %copy-start.6 = (bf16[1024,128]{1,0:T(8,128)(2,1)S(1)}, bf16[1024,128]{1,0:T(8,128)(2,1)}, u32[]{:S(2)}) copy-start(bf16[1024,128]{1,0:T(8,128)(2,1)} %convolution_convert_fusion.5) | copy-start | bytes 786436
  84.9 12.2 %copy-start.8 = (bf16[1024,128]{1,0:T(8,128)(2,1)S(1)}, bf16[1024,128]{1,0:T(8,128)(2,1)}, u32[]{:S(2)}) copy-start(bf16[1024,128]{1,0:T(8,128)(2,1)} %convolution_convert_fusion.6) | copy-start | bytes 786436
  84.9 12.3 %copy-start.9 = (bf16[1024,128]{1,0:T(8,128)(2,1)S(1)}, bf16[1024,128]{1,0:T(8,128)(2,1)}, u32[]{:S(2)}) copy-start(bf16[1024,128]{1,0:T(8,128)(2,1)} %convolution_convert_fusion.3) | copy-start | bytes 786436
  86.0 17.5 %all-to-all-start.2 = ((bf16[1,32,32,128]{3,2,0,1:T(8,128)(2,1)}), bf16[1,32,32,128]{3,2,0,1:T(8,128)(2,1)}, u32[]{:S(2)}, u32[]{:S(2)}) async-start(bf16[1,32,32,128]{3,2,0,1:T(8,128)(2,1)} %bitcast.30), calls=%async_computation.2 | async-start | bytes 524288 | tf_op jit(solution)/shard_map/all_to_all | solution.py:198
  92.5 8.3 %copy-start.16 = (bf16[8,128,2,64]{1,3,2,0:T(8,128)(2,1)}, bf16[8,128,2,64]{1,3,2,0:T(8,128)(2,1)S(1)}, u32[]{:S(2)}) copy-start(bf16[8,128,2,64]{1,3,2,0:T(8,128)(2,1)S(1)} %copy.276) | copy-start | bytes 786436
  95.2 2.9 copy-start.21
  98.1 2.7 copy-start.19
  102.3 14.1 %copy-start.17 = (bf16[8,128,2,64]{1,3,2,0:T(8,128)(2,1)S(1)}, bf16[8,128,2,64]{1,3,2,0:T(8,128)(2,1)}, u32[]{:S(2)}) copy-start(bf16[8,128,2,64]{1,3,2,0:T(8,128)(2,1)} %copy-done.16) | copy-start | bytes 786436
  103.5 31.0 %all-to-all-start.1 = ((bf16[1,32,96,128]{3,2,0,1:T(8,128)(2,1)}), bf16[1,32,96,128]{3,2,0,1:T(8,128)(2,1)S(1)}, u32[]{:S(2)}, u32[]{:S(2)}) async-start(bf16[1,32,96,128]{3,2,0,1:T(8,128)(2,1)} %pad_maximum_fusion.1), calls=%async_computation.1 | async-start | bytes 1572864 | tf_op jit(solution)/shard_map/all_to_all | solution.py:30
  135.3 1.3 copy-start.33
  135.3 2.1 copy-start.32
  137.4 3.8 copy-start.26
  137.8 5.0 %copy-start.10 = (f32[8,2,128,64]{2,3,1,0:T(8,128)S(1)}, f32[8,2,128,64]{2,3,1,0:T(8,128)}, u32[]{:S(2)}) copy-start(f32[8,2,128,64]{2,3,1,0:T(8,128)} %copy.382) | copy-start | bytes 1572868
  141.2 3.4 copy-start.23
  141.2 3.4 copy-start.24
  141.2 3.4 copy-start.31
  144.7 1.2 copy-start.30
  145.1 0.8 copy-start.14
  145.9 13.5 %copy-start.18 = (bf16[8,128,2,64]{1,3,2,0:T(8,128)(2,1)S(1)}, bf16[8,128,2,64]{1,3,2,0:T(8,128)(2,1)}, u32[]{:S(2)}) copy-start(bf16[8,128,2,64]{1,3,2,0:T(8,128)(2,1)} %copy-done.16) | copy-start | bytes 786436
  151.1 48.4 %all-to-all-start.4 = ((bf16[32,1,32,128]{3,2,1,0:T(8,128)(2,1)}), bf16[32,1,32,128]{3,2,1,0:T(8,128)(2,1)}, u32[]{:S(2)}, u32[]{:S(2)}) async-start(bf16[32,1,32,128]{3,2,1,0:T(8,128)(2,1)} %copy.333), calls=%async_computation.4 | async-start | bytes 524288 | tf_op jit(solution)/shard_map/all_to_all | solution.py:202
  159.4 2.6 copy-start.35
  163.3 7.5 %copy-start.12 = (f32[8,128,2,64]{1,3,2,0:T(8,128)S(1)}, f32[8,128,2,64]{1,3,2,0:T(8,128)}, u32[]{:S(2)}) copy-start(f32[8,128,2,64]{1,3,2,0:T(8,128)} %convolution_bitcast_fusion.3) | copy-start | bytes 1572868
  172.1 7.5 %copy-start.11 = (f32[8,128,2,64]{1,3,2,0:T(8,128)S(1)}, f32[8,128,2,64]{1,3,2,0:T(8,128)}, u32[]{:S(2)}) copy-start(f32[8,128,2,64]{1,3,2,0:T(8,128)} %convolution_bitcast_fusion.5) | copy-start | bytes 1572868
  180.9 7.5 %copy-start.25 = (bf16[8,128,2,64]{1,3,2,0:T(8,128)(2,1)S(1)}, bf16[8,128,2,64]{1,3,2,0:T(8,128)(2,1)}, u32[]{:S(2)}) copy-start(bf16[8,128,2,64]{1,3,2,0:T(8,128)(2,1)} %copy.313) | copy-start | bytes 786436
  185.8 6.2 %copy-start.15 = (bf16[8,2,128,128]{2,3,1,0:T(8,128)(2,1)S(1)}, bf16[8,2,128,128]{2,3,1,0:T(8,128)(2,1)}, u32[]{:S(2)}) copy-start(bf16[8,2,128,128]{2,3,1,0:T(8,128)(2,1)} %copy-done.14) | copy-start | bytes 1572868
  192.0 4.3 %copy-start.27 = (bf16[8,2,64,128]{3,2,1,0:T(8,128)(2,1)S(1)}, bf16[8,2,64,128]{3,2,1,0:T(8,128)(2,1)}, u32[]{:S(2)}) copy-start(bf16[8,2,64,128]{3,2,1,0:T(8,128)(2,1)} %get-tuple-element.46) | copy-start | bytes 786436
  196.3 17.1 %copy-start.3 = (bf16[32,32,512]{2,1,0:T(8,128)(2,1)S(1)}, bf16[32,32,512]{2,1,0:T(8,128)(2,1)}, u32[]{:S(2)}) copy-start(bf16[32,32,512]{2,1,0:T(8,128)(2,1)} %copy-done.2) | copy-start | bytes 3145732
  199.5 24.6 %all-to-all-start.3 = ((bf16[32,1,32,128]{3,2,1,0:T(8,128)(2,1)}), bf16[32,1,32,128]{3,2,1,0:T(8,128)(2,1)}, u32[]{:S(2)}, u32[]{:S(2)}) async-start(bf16[32,1,32,128]{3,2,1,0:T(8,128)(2,1)} %copy.321), calls=%async_computation.3 | async-start | bytes 524288 | tf_op jit(solution)/shard_map/all_to_all | solution.py:202
  224.0 17.6 %all-to-all-start.5 = ((bf16[32,1,32,128]{3,2,1,0:T(8,128)(2,1)}), bf16[32,1,32,128]{3,2,1,0:T(8,128)(2,1)}, u32[]{:S(2)}, u32[]{:S(2)}) async-start(bf16[32,1,32,128]{3,2,1,0:T(8,128)(2,1)} %copy.345), calls=%async_computation.5 | async-start | bytes 524288 | tf_op jit(solution)/shard_map/all_to_all | solution.py:202
  231.0 0.7 copy-start.28
  241.7 17.6 %all-to-all-start.9 = ((bf16[32,1,32,128]{3,2,1,0:T(8,128)(2,1)}), bf16[32,1,32,128]{3,2,1,0:T(8,128)(2,1)}, u32[]{:S(2)}, u32[]{:S(2)}) async-start(bf16[32,1,32,128]{3,2,1,0:T(8,128)(2,1)} %copy.353), calls=%async_computation.9 | async-start | bytes 524288 | tf_op jit(solution)/shard_map/all_to_all | solution.py:202
  248.6 0.7 copy-start.29
  259.3 50.0 %all-to-all-start.6 = ((bf16[8,1024,128]{1,2,0:T(8,128)(2,1)}), bf16[8,1024,128]{1,2,0:T(8,128)(2,1)}, u32[]{:S(2)}, u32[]{:S(2)}) async-start(bf16[8,1024,128]{1,2,0:T(8,128)(2,1)} %bitcast.203), calls=%async_computation.6 | async-start | bytes 4194304 | tf_op jit(solution)/shard_map/all_to_all | solution.py:56
  279.9 41.0 %copy-start.34 = (bf16[1,32,32,128]{3,2,1,0:T(8,128)(2,1)S(1)}, bf16[1,32,32,128]{3,2,1,0:T(8,128)(2,1)}, u32[]{:S(2)}) copy-start(bf16[1,32,32,128]{3,2,1,0:T(8,128)(2,1)} %fusion.30) | copy-start | bytes 786436
  313.1 18.8 %all-to-all-start.8 = ((f32[32,1,128]{2,1,0:T(1,128)}), f32[32,1,128]{2,1,0:T(1,128)S(1)}, u32[]{:S(2)}, u32[]{:S(2)}) async-start(f32[32,1,128]{2,1,0:T(1,128)} %broadcast_in_dim.23), calls=%async_computation.8 | async-start | bytes 32768 | tf_op jit(solution)/shard_map/all_to_all | solution.py:62
  332.5 12.5 %all-to-all-start.7 = ((f32[8,1,1024]{2,1,0:T(1,128)}), f32[8,1,1024]{2,1,0:T(1,128)S(1)}, u32[]{:S(2)}, u32[]{:S(2)}) async-start(f32[8,1,1024]{2,1,0:T(1,128)} %broadcast_in_dim.22), calls=%async_computation.7 | async-start | bytes 65536 | tf_op jit(solution)/shard_map/all_to_all | solution.py:62
  345.0 61.5 %all-to-all-start.10 = ((f32[32,32,512]{2,1,0:T(8,128)}), f32[32,32,512]{2,1,0:T(8,128)}, u32[]{:S(2)}, u32[]{:S(2)}) async-start(f32[32,32,512]{2,1,0:T(8,128)} %bitcast.202), calls=%async_computation.10 | async-start | bytes 4194304 | tf_op jit(solution)/shard_map/all_to_all | solution.py:72
